TPU v7x, 32 devices: a whole 2x2x4 slice. The times are simulated.
32 devices in a mesh: rep: 8 (over y, x, core), shard: 4 (over z).
Axes of the slice: x: 2, y: 2, z: 4, core: 2. Of those that a mesh axis runs over, the one named last changes fastest.
Arguments:
- tokens: bfloat16 [4096, 768], P(('rep', 'shard')), may hold values from -30 to 30
- segments: int32 [32, 128], P(('rep', 'shard')), may hold values from 0 to 7, never falling along the last dimension, each value on 1 to 64 neighbouring positions
- w_query: bfloat16 [768, 768], P('shard'), may hold values from -0.21875 to 0.21875
- w_key: bfloat16 [768, 768], P('shard'), may hold values from -0.21875 to 0.21875
- w_value: bfloat16 [768, 768], P('shard'), may hold values from -0.21875 to 0.21875
- w_out: bfloat16 [768, 768], P('shard'), may hold values from -0.875 to 0.875
- b_query: bfloat16 [768], P('shard'), may hold values from -3 to 3
- b_value: bfloat16 [768], P('shard'), may hold values from -3 to 3
- b_out: bfloat16 [768], P('shard'), may hold values from -3 to 3
- gain_one: bfloat16 [768], P('shard'), may hold values from 0.099609375 to 1.8984375
- shift_one: bfloat16 [768], P('shard'), may hold values from -3 to 3
- w_up: bfloat16 [768, 3072], P('shard'), may hold values from -0.21875 to 0.21875
- b_up: bfloat16 [3072], P('shard'), may hold values from -3 to 3
- w_down: bfloat16 [3072, 768], P('shard'), may hold values from -0.109375 to 0.109375
- b_down: bfloat16 [768], P('shard'), may hold values from -3 to 3
- gain_two: bfloat16 [768], P('shard'), may hold values from 0.099609375 to 1.8984375
- shift_two: bfloat16 [768], P('shard'), may hold values from -3 to 3
- cotangent: bfloat16 [4096, 768], P(('rep', 'shard')), may hold values from -6 to 6
Outputs:
- output: bfloat16 [4096, 768], P(('rep', 'shard'))
- grad_tokens: bfloat16 [4096, 768], P(('rep', 'shard'))
- grad_w_query: float32 [768, 768], P('shard')
- grad_w_key: float32 [768, 768], P('shard')
- grad_w_value: float32 [768, 768], P('shard')
- grad_w_out: float32 [768, 768], P('shard')
- grad_b_query: float32 [768], P('shard')
- grad_b_value: float32 [768], P('shard')
- grad_b_out: float32 [768], P('shard')
- grad_gain_one: float32 [768], P('shard')
- grad_shift_one: float32 [768], P('shard')
- grad_w_up: float32 [768, 3072], P('shard')
- grad_b_up: float32 [3072], P('shard')
- grad_w_down: float32 [3072, 768], P('shard')
- grad_b_down: float32 [768], P('shard')
- grad_gain_two: float32 [768], P('shard')
- grad_shift_two: float32 [768], P('shard')
Inputs may be any that keep to these rules, and one draw needn't show every extreme that they name: `segments`: segment numbers never fall along a row; each segment holds 1 to 64 tokens, and in every row exactly one segment holds 64 tokens.
All inputs are finite; a program needn't handle non-finite values.
Results may differ from a plain program's by a relative error of at most 0.014.
The roundings to bfloat16 on the way count: a program that leaves them out, or rounds other values in their place, can miss the bound.
Values may be sent and summed in bfloat16 or wider, within the bound.
A program may use at most 128 MiB of HBM per device.

v0:
```python
import math
import jax
import jax.numpy as jnp
from jax import lax
from jax.sharding import PartitionSpec as P

HEAD_DIM = 64
epsilon = 1e-05
masked_value = -1e30
root_half = 0.7071067811865476
inv_root_tau = 0.3989422804014327


def layer_norm(hidden, gain, shift):
    center = hidden - jnp.mean(hidden, axis=-1, keepdims=True)
    inv_std = lax.rsqrt(jnp.mean(center * center, axis=-1, keepdims=True) + epsilon)
    normed = center * inv_std
    return (normed * gain + shift, normed, inv_std)


def norm_back(upstream, normed, inv_std, gain):
    scaled = upstream * gain
    grad_in = inv_std * (
        scaled
        - jnp.mean(scaled, axis=-1, keepdims=True)
        - normed * jnp.mean(scaled * normed, axis=-1, keepdims=True)
    )
    return (grad_in, jnp.sum(upstream * normed, axis=0), jnp.sum(upstream, axis=0))


def gelu_value(pre):
    return 0.5 * pre * (1.0 + lax.erf(pre * root_half))


def gelu_slope(pre):
    return 0.5 * (1.0 + lax.erf(pre * root_half)) + pre * jnp.exp(-0.5 * pre * pre) * inv_root_tau


def masked_scores(queries, keys, seg_block, scale):
    scores = (
        jnp.einsum("gqhe,gkhe->ghqk", queries, keys, preferred_element_type=jnp.float32) * scale
    )
    allowed = (seg_block[:, :, None] == seg_block[:, None, :])[:, None]
    return jnp.where(allowed, scores, masked_value)


def dense(left, right):
    return jnp.dot(left, right, preferred_element_type=jnp.float32)


def body(
    tokens,
    segments,
    w_query,
    w_key,
    w_value,
    w_out,
    b_query,
    b_value,
    b_out,
    gain_one,
    shift_one,
    w_up,
    b_up,
    w_down,
    b_down,
    gain_two,
    shift_two,
    cotangent,
):
    f32 = jnp.float32
    bf16 = jnp.bfloat16
    fwd_set = (
        lax.all_gather(w_query, "shard", axis=0, tiled=True),
        lax.all_gather(w_key, "shard", axis=0, tiled=True),
        lax.all_gather(w_value, "shard", axis=0, tiled=True),
        lax.all_gather(w_out, "shard", axis=0, tiled=True),
        lax.all_gather(b_query, "shard", axis=0, tiled=True),
        lax.all_gather(b_value, "shard", axis=0, tiled=True),
        lax.all_gather(b_out, "shard", axis=0, tiled=True),
        lax.all_gather(gain_one, "shard", axis=0, tiled=True),
        lax.all_gather(shift_one, "shard", axis=0, tiled=True),
        lax.all_gather(w_up, "shard", axis=0, tiled=True),
        lax.all_gather(b_up, "shard", axis=0, tiled=True),
        lax.all_gather(w_down, "shard", axis=0, tiled=True),
        lax.all_gather(b_down, "shard", axis=0, tiled=True),
        lax.all_gather(gain_two, "shard", axis=0, tiled=True),
        lax.all_gather(shift_two, "shard", axis=0, tiled=True),
    )
    (
        full_query,
        full_key,
        full_value,
        full_out,
        bias_query,
        bias_value,
        bias_out,
        full_gain_one,
        full_shift_one,
        full_up,
        bias_up,
        full_down,
        bias_down,
        full_gain_two,
        full_shift_two,
    ) = fwd_set
    rows_here, seq_len = segments.shape
    width = tokens.shape[1]
    heads_count = width // HEAD_DIM
    scale = 1.0 / math.sqrt(HEAD_DIM)

    def split_heads(matrix):
        return matrix.reshape(rows_here, seq_len, heads_count, HEAD_DIM)

    queries = (dense(tokens, full_query) + bias_query.astype(f32)).astype(bf16)
    keys = dense(tokens, full_key).astype(bf16)
    values = (dense(tokens, full_value) + bias_value.astype(f32)).astype(bf16)
    q_heads, k_heads, v_heads = (split_heads(queries), split_heads(keys), split_heads(values))
    scores = masked_scores(q_heads, k_heads, segments, scale)
    top = jnp.max(scores, axis=-1, keepdims=True)
    log_total = top + jnp.log(jnp.sum(jnp.exp(scores - top), axis=-1, keepdims=True))
    probs = jnp.exp(scores - log_total).astype(bf16)
    context = (
        jnp.einsum("ghqk,gkhe->gqhe", probs, v_heads, preferred_element_type=f32)
        .astype(bf16)
        .reshape(-1, width)
    )
    resid_one = tokens.astype(f32) + dense(context, full_out) + bias_out.astype(f32)
    norm_one, normed_one, inv_one = layer_norm(
        resid_one, full_gain_one.astype(f32), full_shift_one.astype(f32)
    )
    norm_one_b = norm_one.astype(bf16)
    pre_act = dense(norm_one_b, full_up) + bias_up.astype(f32)
    act = gelu_value(pre_act).astype(bf16)
    resid_two = norm_one + dense(act, full_down) + bias_down.astype(f32)
    final, normed_two, inv_two = layer_norm(
        resid_two, full_gain_two.astype(f32), full_shift_two.astype(f32)
    )
    output = final.astype(bf16)
    back_query, back_key, back_value, back_out = (full_query, full_key, full_value, full_out)
    back_up, back_down, back_gain_one, back_gain_two = (
        full_up,
        full_down,
        full_gain_one,
        full_gain_two,
    )
    g_resid_two, g_gain_two, g_shift_two = norm_back(
        cotangent.astype(f32), normed_two, inv_two, back_gain_two.astype(f32)
    )
    g_two_b = g_resid_two.astype(bf16)
    g_b_down = jnp.sum(g_resid_two, axis=0)
    g_pre = dense(g_two_b, back_down.T) * gelu_slope(pre_act)
    g_b_up = jnp.sum(g_pre, axis=0)
    g_pre_b = g_pre.astype(bf16)
    g_norm_one = g_resid_two + dense(g_pre_b, back_up.T)
    g_resid_one, g_gain_one, g_shift_one = norm_back(
        g_norm_one, normed_one, inv_one, back_gain_one.astype(f32)
    )
    g_one_b = g_resid_one.astype(bf16)
    g_b_out = jnp.sum(g_resid_one, axis=0)
    g_context = split_heads(dense(g_one_b, back_out.T).astype(bf16))
    probs_f = jnp.exp(masked_scores(q_heads, k_heads, segments, scale) - log_total)
    probs_b = probs_f.astype(bf16)
    g_probs = jnp.einsum("gqhe,gkhe->ghqk", g_context, v_heads, preferred_element_type=f32)
    delta = jnp.sum(probs_f * g_probs, axis=-1, keepdims=True)
    g_scores = (probs_f * (g_probs - delta) * scale).astype(bf16)
    g_queries = jnp.einsum(
        "ghqk,gkhe->gqhe", g_scores, k_heads, preferred_element_type=f32
    ).reshape(-1, width)
    g_keys = jnp.einsum("ghqk,gqhe->gkhe", g_scores, q_heads, preferred_element_type=f32).reshape(
        -1, width
    )
    g_values = jnp.einsum(
        "ghqk,gqhe->gkhe", probs_b, g_context, preferred_element_type=f32
    ).reshape(-1, width)
    g_b_query = jnp.sum(g_queries, axis=0)
    g_b_value = jnp.sum(g_values, axis=0)
    gq_b, gk_b, gv_b = (g_queries.astype(bf16), g_keys.astype(bf16), g_values.astype(bf16))
    grad_tokens = (
        g_resid_one
        + dense(gq_b, back_query.T)
        + dense(gk_b, back_key.T)
        + dense(gv_b, back_value.T)
    ).astype(bf16)
    columns = (
        lax.all_to_all(tokens, "shard", split_axis=1, concat_axis=0, tiled=True),
        lax.all_to_all(context, "shard", split_axis=1, concat_axis=0, tiled=True),
        lax.all_to_all(norm_one_b, "shard", split_axis=1, concat_axis=0, tiled=True),
        lax.all_to_all(act, "shard", split_axis=1, concat_axis=0, tiled=True),
    )
    gathered = (
        lax.all_gather(gq_b, "shard", axis=0, tiled=True),
        lax.all_gather(gk_b, "shard", axis=0, tiled=True),
        lax.all_gather(gv_b, "shard", axis=0, tiled=True),
        lax.all_gather(g_one_b, "shard", axis=0, tiled=True),
        lax.all_gather(g_pre_b, "shard", axis=0, tiled=True),
        lax.all_gather(g_two_b, "shard", axis=0, tiled=True),
    )
    vectors = (
        lax.psum_scatter(
            g_b_query.astype(jnp.bfloat16), "shard", scatter_dimension=0, tiled=True
        ).astype(jnp.float32),
        lax.psum_scatter(
            g_b_value.astype(jnp.bfloat16), "shard", scatter_dimension=0, tiled=True
        ).astype(jnp.float32),
        lax.psum_scatter(
            g_b_out.astype(jnp.bfloat16), "shard", scatter_dimension=0, tiled=True
        ).astype(jnp.float32),
        lax.psum_scatter(
            g_gain_one.astype(jnp.bfloat16), "shard", scatter_dimension=0, tiled=True
        ).astype(jnp.float32),
        lax.psum_scatter(
            g_shift_one.astype(jnp.bfloat16), "shard", scatter_dimension=0, tiled=True
        ).astype(jnp.float32),
        lax.psum_scatter(
            g_b_up.astype(jnp.bfloat16), "shard", scatter_dimension=0, tiled=True
        ).astype(jnp.float32),
        lax.psum_scatter(
            g_b_down.astype(jnp.bfloat16), "shard", scatter_dimension=0, tiled=True
        ).astype(jnp.float32),
        lax.psum_scatter(
            g_gain_two.astype(jnp.bfloat16), "shard", scatter_dimension=0, tiled=True
        ).astype(jnp.float32),
        lax.psum_scatter(
            g_shift_two.astype(jnp.bfloat16), "shard", scatter_dimension=0, tiled=True
        ).astype(jnp.float32),
    )
    own_query = dense(columns[0].T, gathered[0])
    own_key = dense(columns[0].T, gathered[1])
    own_value = dense(columns[0].T, gathered[2])
    own_out = dense(columns[1].T, gathered[3])
    own_up = dense(columns[2].T, gathered[4])
    own_down = dense(columns[3].T, gathered[5])
    summed = lax.psum(
        (
            own_query,
            own_key,
            own_value,
            own_out,
            vectors[0],
            vectors[1],
            vectors[2],
            vectors[3],
            vectors[4],
            own_up,
            vectors[5],
            own_down,
            vectors[6],
            vectors[7],
            vectors[8],
        ),
        "rep",
    )
    return (
        output,
        grad_tokens,
        summed[0],
        summed[1],
        summed[2],
        summed[3],
        summed[4],
        summed[5],
        summed[6],
        summed[7],
        summed[8],
        summed[9],
        summed[10],
        summed[11],
        summed[12],
        summed[13],
        summed[14],
    )


def solution(mesh):
    return jax.shard_map(
        body,
        mesh=mesh,
        in_specs=(
            P(("rep", "shard"), None),
            P(("rep", "shard"), None),
            P("shard", None),
            P("shard", None),
            P("shard", None),
            P("shard", None),
            P("shard"),
            P("shard"),
            P("shard"),
            P("shard"),
            P("shard"),
            P("shard", None),
            P("shard"),
            P("shard", None),
            P("shard"),
            P("shard"),
            P("shard"),
            P(("rep", "shard"), None),
        ),
        out_specs=(
            P(("rep", "shard"), None),
            P(("rep", "shard"), None),
            P("shard", None),
            P("shard", None),
            P("shard", None),
            P("shard", None),
            P("shard"),
            P("shard"),
            P("shard"),
            P("shard"),
            P("shard"),
            P("shard", None),
            P("shard"),
            P("shard", None),
            P("shard"),
            P("shard"),
            P("shard"),
        ),
        check_vma=False,
    )
```

profile of v0, /device:TPU:0, one launch (start us, length us, event | category | flops | bytes accessed | tf_op | source)
XLA Modules:
  0.0 633.8 jit_solution(14550670519471130721)
XLA Ops:
  12.1 6.3 %all-to-all-start = ((bf16[128,4,192]{0,2,1:T(8,128)(2,1)}), bf16[128,4,192]{0,2,1:T(8,128)(2,1)S(1)}, u32[]{:S(2)}, u32[]{:S(2)}) async-start(bf16[128,4,192]{0,2,1:T(8,128)(2,1)} %bitcast.19), calls=%async_computation | async-start | bytes 393216 | tf_op jit(solution)/shard_map/all_to_all | solution.py:186
  21.4 20.4 %all-reduce.20 = (bf16[768]{0:T(1024)(128)(2,1)S(1)}, bf16[768]{0:T(1024)(128)(2,1)S(1)}, bf16[768]{0:T(1024)(128)(2,1)S(1)}, bf16[768]{0:T(1024)(128)(2,1)S(1)}...) all-reduce(bf16[768]{0:T(1024)(128)(2,1)S(1)} %dynamic-update-slice, ...), channel_id=1, replica_groups=mesh['rep'=8,'shard'=4] {'shard'}, use_global_device_ids=true, to_apply=%add | all-reduce | flops 5376 | bytes 21504
  41.8 13.3 %all-gather = bf16[4,1,768]{2,1,0:T(2,128)(2,1)S(1)} all-gather(bf16[1,1,768]{2,1,0:T(2,128)(2,1)S(1)} %reshape.263), channel_id=1, replica_groups=mesh['rep'=8,'shard'=4] {'shard'}, dimensions={0}, use_global_device_ids=true | all-gather | bytes 7680 | tf_op jit(solution)/shard_map/all_gather | solution.py:84
  55.3 1.6 fusion.13
  57.0 19.7 %all-gather.13.cloned.1.call-done = bf16[768,768]{1,0:T(8,128)(2,1)} async-done(((bf16[192,768]{1,0:T(8,128)(2,1)}), bf16[768,768]{1,0:T(8,128)(2,1)}) %all-gather.13.cloned.1.call-update) | async-done | bytes 1179664 | tf_op jit(solution)/shard_map/all_gather | solution.py:75
  76.8 1.6 convolution_convert_fusion.3
  78.5 29.3 %all-gather.9.cloned.1.call-done = bf16[768,768]{1,0:T(8,128)(2,1)} async-done(((bf16[192,768]{1,0:T(8,128)(2,1)}), bf16[768,768]{1,0:T(8,128)(2,1)}) %all-gather.9.cloned.1.call-update) | async-done | bytes 1179664 | tf_op jit(solution)/shard_map/all_gather | solution.py:76
  107.9 1.6 fusion.12
  111.1 27.7 %all-gather.15.cloned.1.call-done = bf16[768,768]{1,0:T(8,128)(2,1)} async-done(((bf16[192,768]{1,0:T(8,128)(2,1)}), bf16[768,768]{1,0:T(8,128)(2,1)}) %all-gather.15.cloned.1.call-update) | async-done | bytes 1179664 | tf_op jit(solution)/shard_map/all_gather | solution.py:77
  138.8 1.8 fusion.60
  141.8 87.0 %all-gather.17.cloned.1.call-done = bf16[768,3072]{1,0:T(8,128)(2,1)} async-done(((bf16[192,3072]{1,0:T(8,128)(2,1)}), bf16[768,3072]{1,0:T(8,128)(2,1)}) %all-gather.17.cloned.1.call-update) | async-done | bytes 4718608 | tf_op jit(solution)/shard_map/all_gather | solution.py:83
  228.9 4.6 multiply_convert_fusion
  233.4 84.7 %all-gather.19.cloned.1.call-done = bf16[3072,768]{1,0:T(8,128)(2,1)} async-done(((bf16[768,768]{1,0:T(8,128)(2,1)}), bf16[3072,768]{1,0:T(8,128)(2,1)}) %all-gather.19.cloned.1.call-update) | async-done | bytes 4718608 | tf_op jit(solution)/shard_map/all_gather | solution.py:85
  318.1 3.4 fusion.61
  323.4 3.2 fusion.55
  326.6 5.0 multiply_reduce_fusion.1
  331.6 1.5 fusion.54
  335.9 1.7 fusion.57
  338.4 34.3 %all_gather.79 = bf16[512,768]{0,1:T(8,128)(2,1)S(1)} all-gather(bf16[128,768]{0,1:T(8,128)(2,1)S(1)} %bitcast.132), channel_id=1, replica_groups=mesh['rep'=8,'shard'=4] {'shard'}, dimensions={0}, use_global_device_ids=true | all-gather | bytes 983040 | tf_op jit(solution)/shard_map/all_gather | solution.py:193
  372.7 10.4 %all-to-all-start.1 = ((bf16[128,4,192]{0,2,1:T(8,128)(2,1)}), bf16[128,4,192]{0,2,1:T(8,128)(2,1)}, u32[]{:S(2)}, u32[]{:S(2)}) async-start(bf16[128,4,192]{0,2,1:T(8,128)(2,1)} %bitcast.27), calls=%async_computation.1 | async-start | bytes 393216 | tf_op jit(solution)/shard_map/all_to_all | solution.py:187
  384.4 32.5 %all_gather.80 = bf16[512,768]{0,1:T(8,128)(2,1)S(1)} all-gather(bf16[128,768]{0,1:T(8,128)(2,1)S(1)} %bitcast.126), channel_id=1, replica_groups=mesh['rep'=8,'shard'=4] {'shard'}, dimensions={0}, use_global_device_ids=true | all-gather | bytes 983040 | tf_op jit(solution)/shard_map/all_gather | solution.py:194
  416.9 17.8 %all_gather.78 = bf16[512,768]{0,1:T(8,128)(2,1)S(1)} all-gather(bf16[128,768]{0,1:T(8,128)(2,1)} %bitcast.134), channel_id=1, replica_groups=mesh['rep'=8,'shard'=4] {'shard'}, dimensions={0}, use_global_device_ids=true | all-gather | bytes 983040 | tf_op jit(solution)/shard_map/all_gather | solution.py:192
  434.7 3.5 all-to-all-start.3
  438.2 1.2 convolution_bitcast_fusion
  440.6 30.5 %all_gather.81 = bf16[512,768]{1,0:T(8,128)(2,1)S(1)} all-gather(bf16[128,768]{1,0:T(8,128)(2,1)S(1)} %copy-done.8), channel_id=1, replica_groups=mesh['rep'=8,'shard'=4] {'shard'}, dimensions={0}, use_global_device_ids=true | all-gather | bytes 983040 | tf_op jit(solution)/shard_map/all_gather | solution.py:195
  471.1 2.1 fusion.37
  473.2 17.2 %all_gather.83 = bf16[512,768]{1,0:T(8,128)(2,1)S(1)} all-gather(bf16[128,768]{1,0:T(8,128)(2,1)S(1)} %copy-done.19), channel_id=1, replica_groups=mesh['rep'=8,'shard'=4] {'shard'}, dimensions={0}, use_global_device_ids=true | all-gather | bytes 983040 | tf_op jit(solution)/shard_map/all_gather | solution.py:197
  490.4 5.3 all-to-all-start.2
  495.8 2.2 fusion.65
  498.0 4.0 all-to-all-done.2
  502.0 4.1 fusion.34
  509.6 1.3 dynamic-update-slice.7
  512.3 18.8 %all-reduce.19 = (bf16[768]{0:T(1024)(128)(2,1)}, bf16[768]{0:T(1024)(128)(2,1)}, bf16[768]{0:T(1024)(128)(2,1)}, bf16[768]{0:T(1024)(128)(2,1)}, bf16[768]{0:T(...) all-reduce(bf16[768]{0:T(1024)(128)(2,1)} %dynamic-update-slice.7, ...), channel_id=1, replica_groups=mesh['rep'=8,'shard'=4] {'shard'}, use_global_device_ids=true, to_apply=%add.7 | all-reduce | flops 9984 | bytes 39936
  531.8 1.3 dynamic-slice_convert_fusion.1
  533.1 1.3 dynamic-slice_convert_fusion.2
  534.4 1.3 dynamic-slice_convert_fusion.3
  535.7 1.3 dynamic-slice_convert_fusion.4
  537.1 1.3 dynamic-slice_convert_fusion.5
  538.4 1.3 dynamic-slice_convert_fusion.6
  539.7 1.3 dynamic-slice_convert_fusion.7
  541.0 1.3 dynamic-slice_convert_fusion.8
  543.1 23.2 %all-reduce.17 = (f32[192]{0:T(256)}, f32[192]{0:T(256)}, f32[192]{0:T(256)}, f32[192]{0:T(256)}, f32[192]{0:T(256)}, /*index=5*/f32[768]{0:T(1024)}, f32[192]{0:T(256)}, f32[192]{0:T(256)}, f32[192]{0:T(256)}) all-reduce(f32[192]{0:T(256)} %dynamic-slice_convert_fusion.8, ...), channel_id=1, replica_groups=mesh['rep'=8,'shard'=4] {'rep'}, use_global_device_ids=true, to_apply=%region_17.18 | all-reduce | flops 2304 | bytes 18432 | tf_op jit(solution)/shard_map/psum | solution.py:234
  566.3 1.5 add_convert_fusion
  567.8 1.5 convolution_add_fusion.3
  571.9 46.6 %all-reduce.23.cloned.1.call-done = (f32[192,768]{1,0:T(8,128)}, f32[192,768]{1,0:T(8,128)}, f32[192,768]{1,0:T(8,128)}, f32[192,768]{1,0:T(8,128)}, f32[192,3072]{1,0:T(8,128)}, /*index=5*/f32[768,768]{1,0:T(8,128)}) async-done(((f32[192,768]{1,0:T(8,128)}, f32[192,768]{1,0:T(8,128)}, f32[192,768]{1,0:T(8,128)}, f32[192,768]{1,0:T(8,128)}, f32[192,3072]{1,0:T(8,128)}, /*index=5*/f32[768,768]{1,0:T(8,128)}), ...) | async-done | bytes 7077904 | tf_op jit(solution)/shard_map/psum | solution.py:234
  618.5 2.0 copy.120
  623.0 1.4 copy.124
  625.5 1.4 copy.125
  (171 shorter events, 29.1 us)
Async XLA Ops:
  7.2 48.1 %all-gather.11.cloned.1.call-start = ((), (), s32[]{:S(2)}) async-start(), calls=%async_computation.5 | async-start | bytes 1474560 | tf_op jit(solution)/shard_map/all_gather | solution.py:74
  7.9 3.3 copy-start
  7.9 68.8 %all-gather.13.cloned.1.call-start = ((), (), s32[]{:S(2)}) async-start(), calls=%async_computation.6 | async-start | bytes 1474560 | tf_op jit(solution)/shard_map/all_gather | solution.py:75
  8.7 99.2 %all-gather.9.cloned.1.call-start = ((), (), s32[]{:S(2)}) async-start(), calls=%async_computation.4 | async-start | bytes 1474560 | tf_op jit(solution)/shard_map/all_gather | solution.py:76
  9.4 129.4 %all-gather.15.cloned.1.call-start = ((), (), s32[]{:S(2)}) async-start(), calls=%async_computation.7 | async-start | bytes 1474560 | tf_op jit(solution)/shard_map/all_gather | solution.py:77
  10.0 8.4 %copy-start.30 = (u32[32]{0:T(128)S(1)}, u32[32]{0:T(128)}, u32[]{:S(2)}) copy-start(u32[32]{0:T(128)} %constant.35) | copy-start | bytes 388
  10.0 9.7 %copy-start.32 = (bf16[192]{0:T(256)(128)(2,1)S(1)}, bf16[192]{0:T(256)(128)(2,1)}, u32[]{:S(2)}) copy-start(bf16[192]{0:T(256)(128)(2,1)} %param.25) | copy-start | bytes 1156
  10.0 9.9 %copy-start.33 = (bf16[192]{0:T(256)(128)(2,1)S(1)}, bf16[192]{0:T(256)(128)(2,1)}, u32[]{:S(2)}) copy-start(bf16[192]{0:T(256)(128)(2,1)} %param.24) | copy-start | bytes 1156
  10.0 10.2 %copy-start.34 = (bf16[192]{0:T(256)(128)(2,1)S(1)}, bf16[192]{0:T(256)(128)(2,1)}, u32[]{:S(2)}) copy-start(bf16[192]{0:T(256)(128)(2,1)} %param.26) | copy-start | bytes 1156
  10.0 10.4 %copy-start.35 = (bf16[192]{0:T(256)(128)(2,1)S(1)}, bf16[192]{0:T(256)(128)(2,1)}, u32[]{:S(2)}) copy-start(bf16[192]{0:T(256)(128)(2,1)} %param.27) | copy-start | bytes 1156
  10.1 10.6 %copy-start.36 = (bf16[192]{0:T(256)(128)(2,1)S(1)}, bf16[192]{0:T(256)(128)(2,1)}, u32[]{:S(2)}) copy-start(bf16[192]{0:T(256)(128)(2,1)} %param.28) | copy-start | bytes 1156
  10.1 10.8 %copy-start.37 = (bf16[192]{0:T(256)(128)(2,1)S(1)}, bf16[192]{0:T(256)(128)(2,1)}, u32[]{:S(2)}) copy-start(bf16[192]{0:T(256)(128)(2,1)} %param.32) | copy-start | bytes 1156
  10.1 11.1 %copy-start.38 = (bf16[192]{0:T(256)(128)(2,1)S(1)}, bf16[192]{0:T(256)(128)(2,1)}, u32[]{:S(2)}) copy-start(bf16[192]{0:T(256)(128)(2,1)} %param.33) | copy-start | bytes 1156
  10.1 31.7 %copy-start.31 = (bf16[768]{0:T(1024)(128)(2,1)S(1)}, bf16[768]{0:T(1024)(128)(2,1)}, u32[]{:S(2)}) copy-start(bf16[768]{0:T(1024)(128)(2,1)} %param.30) | copy-start | bytes 4612
  10.1 45.0 %copy-start.29 = (s32[1,128]{1,0:T(1,128)S(1)}, s32[1,128]{1,0:T(1,128)}, u32[]{:S(2)}) copy-start(s32[1,128]{1,0:T(1,128)} %param.19) | copy-start | bytes 1540
  10.1 218.8 %all-gather.17.cloned.1.call-start = ((), (), s32[]{:S(2)}) async-start(), calls=%async_computation.8 | async-start | bytes 5898240 | tf_op jit(solution)/shard_map/all_gather | solution.py:83
  10.7 307.4 %all-gather.19.cloned.1.call-start = ((), (), s32[]{:S(2)}) async-start(), calls=%async_computation.9 | async-start | bytes 5898240 | tf_op jit(solution)/shard_map/all_gather | solution.py:85
  12.1 360.6 %all-to-all-start = ((bf16[128,4,192]{0,2,1:T(8,128)(2,1)}), bf16[128,4,192]{0,2,1:T(8,128)(2,1)S(1)}, u32[]{:S(2)}, u32[]{:S(2)}) async-start(bf16[128,4,192]{0,2,1:T(8,128)(2,1)} %bitcast.19), calls=%async_computation | async-start | bytes 393216 | tf_op jit(solution)/shard_map/all_to_all | solution.py:186
  18.4 483.6 %all-gather.21.cloned.1.call-start = ((), (), s32[]{:S(2)}) async-start(), calls=%async_computation.10 | async-start | bytes 3932160 | tf_op jit(solution)/shard_map/all_gather | solution.py:196
  57.0 52.6 %copy-start.12 = (bf16[128,768]{0,1:T(8,128)(2,1)}, bf16[128,768]{0,1:T(8,128)(2,1)S(1)}, u32[]{:S(2)}) copy-start(bf16[128,768]{0,1:T(8,128)(2,1)S(1)} %copy.62) | copy-start | bytes 589828
  78.5 31.5 %copy-start.14 = (bf16[128,768]{0,1:T(8,128)(2,1)}, bf16[128,768]{0,1:T(8,128)(2,1)S(1)}, u32[]{:S(2)}) copy-start(bf16[128,768]{0,1:T(8,128)(2,1)S(1)} %copy.63) | copy-start | bytes 589828
  140.7 185.9 %copy-start.23 = (f32[128]{0:T(128)}, f32[128]{0:T(128)S(1)}, u32[]{:S(2)}) copy-start(f32[128]{0:T(128)S(1)} %broadcast_multiply_fusion.5) | copy-start | bytes 1540
  140.9 185.7 %copy-start.26 = (f32[128]{0:T(128)}, f32[128]{0:T(128)S(1)}, u32[]{:S(2)}) copy-start(f32[128]{0:T(128)S(1)} %add_rsqrt_fusion.1) | copy-start | bytes 1540
  318.1 5.2 slice-start
  318.1 3.6 copy-start.9
  318.1 5.2 slice-start.1
  321.5 5.0 copy-start.24
  321.7 4.8 copy-start.28
  323.3 3.3 copy-start.18
  331.6 2.3 copy-start.3
  335.5 2.0 copy-start.13
  337.9 46.4 %copy-start.16 = (bf16[12,64,128]{2,1,0:T(8,128)(2,1)}, bf16[12,64,128]{2,1,0:T(8,128)(2,1)S(1)}, u32[]{:S(2)}) copy-start(bf16[12,64,128]{2,1,0:T(8,128)(2,1)S(1)} %convolution_convert_fusion) | copy-start | bytes 589828
  372.7 62.0 %all-to-all-start.1 = ((bf16[128,4,192]{0,2,1:T(8,128)(2,1)}), bf16[128,4,192]{0,2,1:T(8,128)(2,1)}, u32[]{:S(2)}, u32[]{:S(2)}) async-start(bf16[128,4,192]{0,2,1:T(8,128)(2,1)} %bitcast.27), calls=%async_computation.1 | async-start | bytes 393216 | tf_op jit(solution)/shard_map/all_to_all | solution.py:187
  434.7 55.8 %all-to-all-start.3 = ((bf16[128,4,768]{2,0,1:T(8,128)(2,1)}), bf16[128,4,768]{2,0,1:T(8,128)(2,1)S(1)}, u32[]{:S(2)}, u32[]{:S(2)}) async-start(bf16[128,4,768]{2,0,1:T(8,128)(2,1)} %bitcast.117), calls=%async_computation.3 | async-start | bytes 1572864 | tf_op jit(solution)/shard_map/all_to_all | solution.py:189
  438.2 2.5 copy-start.8
  440.6 32.5 %copy-start.19 = (bf16[128,768]{1,0:T(8,128)(2,1)S(1)}, bf16[128,768]{1,0:T(8,128)(2,1)}, u32[]{:S(2)}) copy-start(bf16[128,768]{1,0:T(8,128)(2,1)} %copy-done.18) | copy-start | bytes 589828
  490.4 11.6 %all-to-all-start.2 = ((bf16[128,4,192]{0,2,1:T(8,128)(2,1)}), bf16[128,4,192]{0,2,1:T(8,128)(2,1)S(1)}, u32[]{:S(2)}, u32[]{:S(2)}) async-start(bf16[128,4,192]{0,2,1:T(8,128)(2,1)} %bitcast.31), calls=%async_computation.2 | async-start | bytes 393216 | tf_op jit(solution)/shard_map/all_to_all | solution.py:188
  495.8 122.7 %all-reduce.23.cloned.1.call-start = ((), (), s32[]{:S(2)}) async-start(), calls=%async_computation.11 | async-start | bytes 14155776 | tf_op jit(solution)/shard_map/psum | solution.py:234
  506.1 6.2 copy-start.27
  506.1 60.2 %copy-start.25 = (f32[128]{0:T(128)S(1)}, f32[128]{0:T(128)}, u32[]{:S(2)}) copy-start(f32[128]{0:T(128)} %copy-done.24) | copy-start | bytes 1540
  506.1 61.7 %copy-start.1 = (bf16[768,768]{1,0:T(8,128)(2,1)S(1)}, bf16[768,768]{1,0:T(8,128)(2,1)}, u32[]{:S(2)}) copy-start(bf16[768,768]{1,0:T(8,128)(2,1)} %all-gather.11.cloned.1.call-done) | copy-start | bytes 3538948
  507.0 62.3 %copy-start.2 = (bf16[768,768]{1,0:T(8,128)(2,1)S(1)}, bf16[768,768]{1,0:T(8,128)(2,1)}, u32[]{:S(2)}) copy-start(bf16[768,768]{1,0:T(8,128)(2,1)} %all-gather.13.cloned.1.call-done) | copy-start | bytes 3538948
  507.6 61.7 %copy-start.17 = (bf16[12,64,128]{2,1,0:T(8,128)(2,1)S(1)}, bf16[12,64,128]{2,1,0:T(8,128)(2,1)}, u32[]{:S(2)}) copy-start(bf16[12,64,128]{2,1,0:T(8,128)(2,1)} %copy-done.16) | copy-start | bytes 589828
  618.5 2.1 copy-start.22
  618.5 2.9 copy-start.21
  618.5 3.7 copy-start.20
  620.5 2.5 copy-start.6
  623.0 2.5 copy-start.5
  (5 other events, 6.2 us)
Sparse Core Ops, SparseCore 0:
  9.6 36.2 all-gather.10
  47.4 29.3 all-gather.12
  78.3 29.4 all-gather.8
  109.3 29.4 all-gather.14
  140.2 88.6 all-gather.16
  230.3 87.7 all-gather.18
  326.7 91.0 all-gather.20
  506.2 112.1 all-reduce.22
where the time goes:
time: 635 us; the launch traced here: 634 us
  waiting for transfers between devices  303 us (48%)
  blocking collectives  208 us (33%)
  matrix products  42.7 us (7%)
  starting transfers between devices  25.8 us (4%)
  local copies, waits for them, and re-layouts  19.8 us (3%)
  other arithmetic  17.9 us (3%)
  between operations  16.7 us (3%)
    all_gather x1, waiting for transfers between devices, body(): lax.all_gather(w_up, 'shard', axis=0, tiled=True)  87 us
    all_gather x1, waiting for transfers between devices, body(): lax.all_gather(w_down, 'shard', axis=0, tiled=True)  84.7 us
    psum x1, waiting for transfers between devices, body(): lax.psum((own_query, own_key, own_value, own_out, vectors[0], vectors[1],...  46.6 us
    unnamed x2, blocking collectives  39.2 us
    dot_general x18, matrix products, dense(): return jnp.dot(left, right, preferred_element_type=jnp.float32)  38.6 us
    all_gather x1, blocking collectives, body(): lax.all_gather(gk_b, 'shard', axis=0, tiled=True)  34.3 us
    all_gather x1, blocking collectives, body(): lax.all_gather(gv_b, 'shard', axis=0, tiled=True)  32.5 us
    all_gather x1, blocking collectives, body(): lax.all_gather(g_one_b, 'shard', axis=0, tiled=True)  30.5 us
  transfers between devices with their start and end apart: 12, of which 7 were waited for; matrix products, arithmetic and copies ran while one was open for 10% of the time, Pallas kernels for 0%

commit v1 on v0

--- a/solution.py
+++ b/solution.py
@@ -9,6 +9,19 @@
 masked_value = -1e30
 root_half = 0.7071067811865476
 inv_root_tau = 0.3989422804014327
+
+
+def ring_gather(value, axis, dim):
+    ways = lax.axis_size(axis)
+    up = [(d, (d + 1) % ways) for d in range(ways)]
+    down = [(d, (d - 1) % ways) for d in range(ways)]
+    earlier, later = ([value], [value])
+    for _ in range(ways // 2):
+        earlier.append(lax.ppermute(earlier[-1], axis, up))
+    for _ in range((ways - 1) // 2):
+        later.append(lax.ppermute(later[-1], axis, down))
+    line = jnp.concatenate([*earlier[::-1], *later[1:]], axis=dim)
+    return jnp.roll(line, (lax.axis_index(axis) - ways // 2) * value.shape[dim], axis=dim)
 
 
 def layer_norm(hidden, gain, shift):
@@ -82,7 +95,7 @@
         lax.all_gather(shift_one, "shard", axis=0, tiled=True),
         lax.all_gather(w_up, "shard", axis=0, tiled=True),
         lax.all_gather(b_up, "shard", axis=0, tiled=True),
-        lax.all_gather(w_down, "shard", axis=0, tiled=True),
+        ring_gather(w_down, "shard", 0),
         lax.all_gather(b_down, "shard", axis=0, tiled=True),
         lax.all_gather(gain_two, "shard", axis=0, tiled=True),
         lax.all_gather(shift_two, "shard", axis=0, tiled=True),

time: 635 us -> 601 us (0.946)
  waiting for transfers between devices: 303 us -> 177 us
  blocking collectives: 208 us -> 277 us
  local copies, waits for them, and re-layouts: 19.8 us -> 36.5 us
    all_gather x1 -> x0, waiting for transfers between devices: 84.7 us -> none  [body(): lax.all_gather(w_down, 'shard', axis=0, tiled=True)]
    unnamed x2, blocking collectives: 39.2 us -> 109 us
    all_gather x1, waiting for transfers between devices: 19.7 us -> 0.02 us  [body(): lax.all_gather(w_key, 'shard', axis=0, tiled=True)]
    all_gather x1, waiting for transfers between devices: 87 us -> 70.3 us  [body(): lax.all_gather(w_up, 'shard', axis=0, tiled=True)]
    unnamed x107 -> x110, local copies, waits for them, and re-layouts: 15.9 us -> 30.2 us
  transfers between devices with their start and end apart: 12 -> 14, of which waited for: 7 -> 5; matrix products, arithmetic and copies ran while one was open for 10% -> 14% of each run, Pallas kernels for 0% -> 0%
where the time goes in v1:
time: 601 us; the launch traced here: 600 us
  blocking collectives  277 us (46%)
  waiting for transfers between devices  177 us (29%)
  matrix products  45.1 us (8%)
  local copies, waits for them, and re-layouts  36.5 us (6%)
  starting transfers between devices  28.5 us (5%)
  other arithmetic  17.9 us (3%)
  between operations  16.8 us (3%)
    unnamed x2, blocking collectives  109 us
    all_gather x1, waiting for transfers between devices, body(): lax.all_gather(w_up, 'shard', axis=0, tiled=True)  70.3 us
    psum x1, waiting for transfers between devices, body(): lax.psum((own_query, own_key, own_value, own_out, vectors[0], vectors[1],...  46.7 us
    dot_general x18, matrix products, dense(): return jnp.dot(left, right, preferred_element_type=jnp.float32)  41 us
    all_gather x1, blocking collectives, body(): lax.all_gather(gk_b, 'shard', axis=0, tiled=True)  34.2 us
    all_gather x1, blocking collectives, body(): lax.all_gather(gv_b, 'shard', axis=0, tiled=True)  32.6 us
    all_gather x1, blocking collectives, body(): lax.all_gather(g_one_b, 'shard', axis=0, tiled=True)  30.5 us
    unnamed x110, local copies, waits for them, and re-layouts  30.2 us
  transfers between devices with their start and end apart: 14, of which 5 were waited for; matrix products, arithmetic and copies ran while one was open for 14% of the time, Pallas kernels for 0%

profile of v1, /device:TPU:0, one launch (start us, length us, event | category | flops | bytes accessed | tf_op | source)
XLA Modules:
  0.0 599.6 jit_solution(17770590414227226327)
XLA Ops:
  10.7 3.1 collective-permute-start
  13.8 2.1 collective-permute-start.2
  16.7 3.4 all-to-all-start
  23.1 89.8 %all-reduce.20 = (bf16[768]{0:T(1024)(128)(2,1)S(1)}, bf16[768]{0:T(1024)(128)(2,1)S(1)}, bf16[768]{0:T(1024)(128)(2,1)S(1)}, bf16[768]{0:T(1024)(128)(2,1)S(1)}...) all-reduce(bf16[768]{0:T(1024)(128)(2,1)S(1)} %dynamic-update-slice, ...), channel_id=1, replica_groups=mesh['rep'=8,'shard'=4] {'shard'}, use_global_device_ids=true, to_apply=%add | all-reduce | flops 5376 | bytes 21504
  112.9 13.3 %all-gather = bf16[4,1,768]{2,1,0:T(2,128)(2,1)S(1)} all-gather(bf16[1,1,768]{2,1,0:T(2,128)(2,1)S(1)} %reshape.263), channel_id=1, replica_groups=mesh['rep'=8,'shard'=4] {'shard'}, dimensions={0}, use_global_device_ids=true | all-gather | bytes 7680 | tf_op jit(solution)/shard_map/all_gather | solution.py:97
  126.7 1.6 fusion.25
  128.5 1.7 convolution_convert_fusion.3
  130.3 24.4 %all-gather.8.cloned.1.call-done = bf16[768,768]{1,0:T(8,128)(2,1)} async-done(((bf16[192,768]{1,0:T(8,128)(2,1)}), bf16[768,768]{1,0:T(8,128)(2,1)}) %all-gather.8.cloned.1.call-update) | async-done | bytes 1179664 | tf_op jit(solution)/shard_map/all_gather | solution.py:89
  154.7 1.6 fusion.24
  157.9 28.9 %all-gather.14.cloned.1.call-done = bf16[768,768]{1,0:T(8,128)(2,1)} async-done(((bf16[192,768]{1,0:T(8,128)(2,1)}), bf16[768,768]{1,0:T(8,128)(2,1)}) %all-gather.14.cloned.1.call-update) | async-done | bytes 1179664 | tf_op jit(solution)/shard_map/all_gather | solution.py:90
  186.8 1.8 fusion.74
  189.8 2.4 constant_dynamic-update-slice_fusion.7
  192.2 2.4 constant_dynamic-update-slice_fusion.6
  195.7 2.5 constant_dynamic-update-slice_fusion.4
  198.2 2.4 constant_dynamic-update-slice_fusion.3
  200.6 2.4 constant_dynamic-update-slice_fusion.2
  204.1 2.5 constant_dynamic-update-slice_fusion
  206.6 70.3 %all-gather.16.cloned.1.call-done = bf16[768,3072]{1,0:T(8,128)(2,1)} async-done(((bf16[192,3072]{1,0:T(8,128)(2,1)}), bf16[768,3072]{1,0:T(8,128)(2,1)}) %all-gather.16.cloned.1.call-update) | async-done | bytes 4718608 | tf_op jit(solution)/shard_map/all_gather | solution.py:96
  276.8 3.5 multiply_convert_fusion
  280.3 4.0 fusion.75
  286.1 6.0 %fusion.69 = (bf16[3072]{0:T(1024)(128)(2,1)}, bf16[128,3072]{1,0:T(8,128)(2,1)}) fusion(f32[128,3072]{1,0:T(8,128)S(1)} %get-tuple-element.73, bf16[128,768]{1,0:T(8,128)(2,1)S(1)} %convert_element_type.189, bf16[6144,768]{1,0:T(8,128)(2,1)} %constant_dynamic-update-slice_fusion, s32[]{:T(128)S(6)} %select_n.21), kind=kOutput, calls=%fused_computation.120 | convolution fusion | flops 608302080 | bytes 7280644 | tf_op jit(solution)/shard_map/dot_general | solution.py:61
  292.2 5.0 multiply_reduce_fusion.1
  297.2 1.5 fusion.68
  301.4 1.6 fusion.71
  304.0 34.2 %all_gather.75 = bf16[512,768]{0,1:T(8,128)(2,1)S(1)} all-gather(bf16[128,768]{0,1:T(8,128)(2,1)S(1)} %bitcast.128), channel_id=1, replica_groups=mesh['rep'=8,'shard'=4] {'shard'}, dimensions={0}, use_global_device_ids=true | all-gather | bytes 983040 | tf_op jit(solution)/shard_map/all_gather | solution.py:206
  338.2 10.5 %all-to-all-start.1 = ((bf16[128,4,192]{0,2,1:T(8,128)(2,1)}), bf16[128,4,192]{0,2,1:T(8,128)(2,1)}, u32[]{:S(2)}, u32[]{:S(2)}) async-start(bf16[128,4,192]{0,2,1:T(8,128)(2,1)} %bitcast.27), calls=%async_computation.1 | async-start | bytes 393216 | tf_op jit(solution)/shard_map/all_to_all | solution.py:200
  349.9 32.6 %all_gather.76 = bf16[512,768]{0,1:T(8,128)(2,1)S(1)} all-gather(bf16[128,768]{0,1:T(8,128)(2,1)S(1)} %bitcast.122), channel_id=1, replica_groups=mesh['rep'=8,'shard'=4] {'shard'}, dimensions={0}, use_global_device_ids=true | all-gather | bytes 983040 | tf_op jit(solution)/shard_map/all_gather | solution.py:207
  382.5 17.8 %all_gather.74 = bf16[512,768]{0,1:T(8,128)(2,1)S(1)} all-gather(bf16[128,768]{0,1:T(8,128)(2,1)} %bitcast.130), channel_id=1, replica_groups=mesh['rep'=8,'shard'=4] {'shard'}, dimensions={0}, use_global_device_ids=true | all-gather | bytes 983040 | tf_op jit(solution)/shard_map/all_gather | solution.py:205
  400.2 3.7 all-to-all-start.3
  406.4 30.5 %all_gather.77 = bf16[512,768]{1,0:T(8,128)(2,1)S(1)} all-gather(bf16[128,768]{1,0:T(8,128)(2,1)S(1)} %copy-done.9), channel_id=1, replica_groups=mesh['rep'=8,'shard'=4] {'shard'}, dimensions={0}, use_global_device_ids=true | all-gather | bytes 983040 | tf_op jit(solution)/shard_map/all_gather | solution.py:208
  436.9 2.1 fusion.49
  439.0 17.2 %all_gather.79 = bf16[512,768]{1,0:T(8,128)(2,1)S(1)} all-gather(bf16[128,768]{1,0:T(8,128)(2,1)S(1)} %copy-done.19), channel_id=1, replica_groups=mesh['rep'=8,'shard'=4] {'shard'}, dimensions={0}, use_global_device_ids=true | all-gather | bytes 983040 | tf_op jit(solution)/shard_map/all_gather | solution.py:210
  456.2 5.3 all-to-all-start.2
  461.6 2.2 fusion.79
  463.8 4.0 all-to-all-done.2
  467.8 4.1 fusion.46
  475.4 1.3 dynamic-update-slice.7
  478.2 18.8 %all-reduce.19 = (bf16[768]{0:T(1024)(128)(2,1)}, bf16[768]{0:T(1024)(128)(2,1)}, bf16[768]{0:T(1024)(128)(2,1)}, bf16[768]{0:T(1024)(128)(2,1)}, bf16[768]{0:T(...) all-reduce(bf16[768]{0:T(1024)(128)(2,1)} %dynamic-update-slice.7, ...), channel_id=1, replica_groups=mesh['rep'=8,'shard'=4] {'shard'}, use_global_device_ids=true, to_apply=%add.7 | all-reduce | flops 9984 | bytes 39936
  497.7 1.3 dynamic-slice_convert_fusion.1
  500.3 1.3 dynamic-slice_convert_fusion.3
  505.5 1.3 dynamic-slice_convert_fusion.7
  508.9 23.2 %all-reduce.17 = (f32[192]{0:T(256)}, f32[192]{0:T(256)}, f32[192]{0:T(256)}, f32[192]{0:T(256)}, f32[192]{0:T(256)}, /*index=5*/f32[768]{0:T(1024)}, f32[192]{0:T(256)}, f32[192]{0:T(256)}, f32[192]{0:T(256)}) all-reduce(f32[192]{0:T(256)} %dynamic-slice_convert_fusion.8, ...), channel_id=1, replica_groups=mesh['rep'=8,'shard'=4] {'rep'}, use_global_device_ids=true, to_apply=%region_17.18 | all-reduce | flops 2304 | bytes 18432 | tf_op jit(solution)/shard_map/psum | solution.py:247
  532.1 1.4 add_convert_fusion
  533.5 1.5 convolution_add_fusion.3
  537.6 46.7 %all-reduce.23.cloned.1.call-done = (f32[192,768]{1,0:T(8,128)}, f32[192,768]{1,0:T(8,128)}, f32[192,768]{1,0:T(8,128)}, f32[192,768]{1,0:T(8,128)}, f32[192,3072]{1,0:T(8,128)}, /*index=5*/f32[768,768]{1,0:T(8,128)}) async-done(((f32[192,768]{1,0:T(8,128)}, f32[192,768]{1,0:T(8,128)}, f32[192,768]{1,0:T(8,128)}, f32[192,768]{1,0:T(8,128)}, f32[192,3072]{1,0:T(8,128)}, /*index=5*/f32[768,768]{1,0:T(8,128)}), ...) | async-done | bytes 7077904 | tf_op jit(solution)/shard_map/psum | solution.py:247
  584.3 2.0 copy.127
  588.8 1.4 copy.131
  591.3 1.4 copy.132
  (177 shorter events, 38.9 us)
Async XLA Ops:
  7.2 13.0 %copy-start.30 = (u32[32]{0:T(128)S(1)}, u32[32]{0:T(128)}, u32[]{:S(2)}) copy-start(u32[32]{0:T(128)} %constant.63) | copy-start | bytes 388
  7.2 3.5 copy-start.1
  7.2 8.7 %copy-start = (bf16[128,768]{1,0:T(8,128)(2,1)S(1)}, bf16[128,768]{1,0:T(8,128)(2,1)}, u32[]{:S(2)}) copy-start(bf16[128,768]{1,0:T(8,128)(2,1)} %param.18) | copy-start | bytes 589828
  7.2 14.2 %copy-start.32 = (bf16[192]{0:T(256)(128)(2,1)S(1)}, bf16[192]{0:T(256)(128)(2,1)}, u32[]{:S(2)}) copy-start(bf16[192]{0:T(256)(128)(2,1)} %param.25) | copy-start | bytes 1156
  7.2 14.4 %copy-start.33 = (bf16[192]{0:T(256)(128)(2,1)S(1)}, bf16[192]{0:T(256)(128)(2,1)}, u32[]{:S(2)}) copy-start(bf16[192]{0:T(256)(128)(2,1)} %param.24) | copy-start | bytes 1156
  7.2 14.7 %copy-start.34 = (bf16[192]{0:T(256)(128)(2,1)S(1)}, bf16[192]{0:T(256)(128)(2,1)}, u32[]{:S(2)}) copy-start(bf16[192]{0:T(256)(128)(2,1)} %param.26) | copy-start | bytes 1156
  7.3 14.9 %copy-start.35 = (bf16[192]{0:T(256)(128)(2,1)S(1)}, bf16[192]{0:T(256)(128)(2,1)}, u32[]{:S(2)}) copy-start(bf16[192]{0:T(256)(128)(2,1)} %param.27) | copy-start | bytes 1156
  7.3 15.1 %copy-start.36 = (bf16[192]{0:T(256)(128)(2,1)S(1)}, bf16[192]{0:T(256)(128)(2,1)}, u32[]{:S(2)}) copy-start(bf16[192]{0:T(256)(128)(2,1)} %param.28) | copy-start | bytes 1156
  7.3 15.3 %copy-start.37 = (bf16[192]{0:T(256)(128)(2,1)S(1)}, bf16[192]{0:T(256)(128)(2,1)}, u32[]{:S(2)}) copy-start(bf16[192]{0:T(256)(128)(2,1)} %param.32) | copy-start | bytes 1156
  7.3 15.6 %copy-start.38 = (bf16[192]{0:T(256)(128)(2,1)S(1)}, bf16[192]{0:T(256)(128)(2,1)}, u32[]{:S(2)}) copy-start(bf16[192]{0:T(256)(128)(2,1)} %param.33) | copy-start | bytes 1156
  7.3 105.6 %copy-start.31 = (bf16[768]{0:T(1024)(128)(2,1)S(1)}, bf16[768]{0:T(1024)(128)(2,1)}, u32[]{:S(2)}) copy-start(bf16[768]{0:T(1024)(128)(2,1)} %param.30) | copy-start | bytes 4612
  7.3 119.4 %all-gather.10.cloned.1.call-start = ((), (), s32[]{:S(2)}) async-start(), calls=%async_computation.5 | async-start | bytes 1474560 | tf_op jit(solution)/shard_map/all_gather | solution.py:87
  8.0 118.3 %copy-start.29 = (s32[1,128]{1,0:T(1,128)S(1)}, s32[1,128]{1,0:T(1,128)}, u32[]{:S(2)}) copy-start(s32[1,128]{1,0:T(1,128)} %param.19) | copy-start | bytes 1540
  8.1 120.4 %all-gather.12.cloned.1.call-start = ((), (), s32[]{:S(2)}) async-start(), calls=%async_computation.6 | async-start | bytes 1474560 | tf_op jit(solution)/shard_map/all_gather | solution.py:88
  8.8 145.9 %all-gather.8.cloned.1.call-start = ((), (), s32[]{:S(2)}) async-start(), calls=%async_computation.4 | async-start | bytes 1474560 | tf_op jit(solution)/shard_map/all_gather | solution.py:89
  9.5 177.2 %all-gather.14.cloned.1.call-start = ((), (), s32[]{:S(2)}) async-start(), calls=%async_computation.7 | async-start | bytes 1474560 | tf_op jit(solution)/shard_map/all_gather | solution.py:90
  10.1 266.7 %all-gather.16.cloned.1.call-start = ((), (), s32[]{:S(2)}) async-start(), calls=%async_computation.8 | async-start | bytes 5898240 | tf_op jit(solution)/shard_map/all_gather | solution.py:96
  10.7 115.7 %collective-permute-start = (bf16[768,768]{1,0:T(8,128)(2,1)S(1)}, bf16[768,768]{1,0:T(8,128)(2,1)}, u32[]{:S(2)}, u32[]{:S(2)}) collective-permute-start(bf16[768,768]{1,0:T(8,128)(2,1)S(1)} %copy-done.1), channel_id=1, source_target_pairs={{0,1},{1,2},{2,3},{3,0},{4,5},{5,6},{6,7},{7,4},{8,9},{9,10},{10,1... | collective-permute-start | bytes 3538952 | tf_op jit(solution)/shard_map/ppermute | solution.py:20
  13.8 181.9 %collective-permute-start.2 = (bf16[768,768]{1,0:T(8,128)(2,1)S(1)}, bf16[768,768]{1,0:T(8,128)(2,1)}, u32[]{:S(2)}, u32[]{:S(2)}) collective-permute-start(bf16[768,768]{1,0:T(8,128)(2,1)S(1)} %copy-done.1), channel_id=1, source_target_pairs={{0,3},{1,0},{2,1},{3,2},{4,7},{5,4},{6,5},{7,6},{8,11},{9,8},{10,9... | collective-permute-start | bytes 3538952 | tf_op jit(solution)/shard_map/ppermute | solution.py:22
  16.7 321.5 %all-to-all-start = ((bf16[128,4,192]{0,2,1:T(8,128)(2,1)}), bf16[128,4,192]{0,2,1:T(8,128)(2,1)S(1)}, u32[]{:S(2)}, u32[]{:S(2)}) async-start(bf16[128,4,192]{0,2,1:T(8,128)(2,1)} %bitcast.19), calls=%async_computation | async-start | bytes 393216 | tf_op jit(solution)/shard_map/all_to_all | solution.py:199
  20.1 447.7 %all-gather.18.cloned.1.call-start = ((), (), s32[]{:S(2)}) async-start(), calls=%async_computation.9 | async-start | bytes 3932160 | tf_op jit(solution)/shard_map/all_gather | solution.py:209
  126.4 63.4 %collective-permute-start.1 = (bf16[768,768]{1,0:T(8,128)(2,1)}, bf16[768,768]{1,0:T(8,128)(2,1)}, u32[]{:S(2)}, u32[]{:S(2)}) collective-permute-start(bf16[768,768]{1,0:T(8,128)(2,1)} %collective-permute-done), channel_id=1, source_target_pairs={{0,1},{1,2},{2,3},{3,0},{4,5},{5,6},{6,7},{7,4},{8,9},{9,10},{10,1... | collective-permute-start | bytes 3538952 | tf_op jit(solution)/shard_map/ppermute | solution.py:20
  128.5 28.0 %copy-start.12 = (bf16[128,768]{0,1:T(8,128)(2,1)}, bf16[128,768]{0,1:T(8,128)(2,1)S(1)}, u32[]{:S(2)}) copy-start(bf16[128,768]{0,1:T(8,128)(2,1)S(1)} %copy.62) | copy-start | bytes 589828
  130.3 26.5 %copy-start.14 = (bf16[128,768]{0,1:T(8,128)(2,1)}, bf16[128,768]{0,1:T(8,128)(2,1)S(1)}, u32[]{:S(2)}) copy-start(bf16[128,768]{0,1:T(8,128)(2,1)S(1)} %copy.63) | copy-start | bytes 589828
  188.6 103.6 %copy-start.23 = (f32[128]{0:T(128)}, f32[128]{0:T(128)S(1)}, u32[]{:S(2)}) copy-start(f32[128]{0:T(128)S(1)} %broadcast_multiply_fusion.5) | copy-start | bytes 1540
  188.8 103.4 %copy-start.26 = (f32[128]{0:T(128)}, f32[128]{0:T(128)S(1)}, u32[]{:S(2)}) copy-start(f32[128]{0:T(128)S(1)} %add_rsqrt_fusion.1) | copy-start | bytes 1540
  280.3 4.2 copy-start.10
  284.3 7.9 %copy-start.24 = (f32[128]{0:T(128)}, f32[128]{0:T(128)S(1)}, u32[]{:S(2)}) copy-start(f32[128]{0:T(128)S(1)} %broadcast_multiply_fusion.4) | copy-start | bytes 1540
  284.5 7.6 %copy-start.28 = (f32[128]{0:T(128)}, f32[128]{0:T(128)S(1)}, u32[]{:S(2)}) copy-start(f32[128]{0:T(128)S(1)} %add_rsqrt_fusion) | copy-start | bytes 1540
  286.1 6.1 %copy-start.18 = (bf16[128,768]{1,0:T(8,128)(2,1)}, bf16[128,768]{1,0:T(8,128)(2,1)S(1)}, u32[]{:S(2)}) copy-start(bf16[128,768]{1,0:T(8,128)(2,1)S(1)} %convert_element_type.189) | copy-start | bytes 589828
  297.2 2.3 copy-start.4
  303.5 46.4 %copy-start.16 = (bf16[12,64,128]{2,1,0:T(8,128)(2,1)}, bf16[12,64,128]{2,1,0:T(8,128)(2,1)S(1)}, u32[]{:S(2)}) copy-start(bf16[12,64,128]{2,1,0:T(8,128)(2,1)S(1)} %convolution_convert_fusion) | copy-start | bytes 589828
  338.2 62.0 %all-to-all-start.1 = ((bf16[128,4,192]{0,2,1:T(8,128)(2,1)}), bf16[128,4,192]{0,2,1:T(8,128)(2,1)}, u32[]{:S(2)}, u32[]{:S(2)}) async-start(bf16[128,4,192]{0,2,1:T(8,128)(2,1)} %bitcast.27), calls=%async_computation.1 | async-start | bytes 393216 | tf_op jit(solution)/shard_map/all_to_all | solution.py:200
  400.2 56.0 %all-to-all-start.3 = ((bf16[128,4,768]{2,0,1:T(8,128)(2,1)}), bf16[128,4,768]{2,0,1:T(8,128)(2,1)S(1)}, u32[]{:S(2)}, u32[]{:S(2)}) async-start(bf16[128,4,768]{2,0,1:T(8,128)(2,1)} %bitcast.115), calls=%async_computation.3 | async-start | bytes 1572864 | tf_op jit(solution)/shard_map/all_to_all | solution.py:202
  404.0 2.5 copy-start.9
  406.4 32.5 %copy-start.19 = (bf16[128,768]{1,0:T(8,128)(2,1)S(1)}, bf16[128,768]{1,0:T(8,128)(2,1)}, u32[]{:S(2)}) copy-start(bf16[128,768]{1,0:T(8,128)(2,1)} %copy-done.18) | copy-start | bytes 589828
  456.2 11.6 %all-to-all-start.2 = ((bf16[128,4,192]{0,2,1:T(8,128)(2,1)}), bf16[128,4,192]{0,2,1:T(8,128)(2,1)S(1)}, u32[]{:S(2)}, u32[]{:S(2)}) async-start(bf16[128,4,192]{0,2,1:T(8,128)(2,1)} %bitcast.31), calls=%async_computation.2 | async-start | bytes 393216 | tf_op jit(solution)/shard_map/all_to_all | solution.py:201
  461.5 122.7 %all-reduce.23.cloned.1.call-start = ((), (), s32[]{:S(2)}) async-start(), calls=%async_computation.10 | async-start | bytes 14155776 | tf_op jit(solution)/shard_map/psum | solution.py:247
  471.9 6.3 %copy-start.27 = (bf16[768]{0:T(1024)(128)(2,1)S(1)}, bf16[768]{0:T(1024)(128)(2,1)}, u32[]{:S(2)}) copy-start(bf16[768]{0:T(1024)(128)(2,1)} %get-tuple-element.19) | copy-start | bytes 4612
  471.9 60.2 %copy-start.25 = (f32[128]{0:T(128)S(1)}, f32[128]{0:T(128)}, u32[]{:S(2)}) copy-start(f32[128]{0:T(128)} %copy-done.24) | copy-start | bytes 1540
  471.9 61.7 %copy-start.2 = (bf16[768,768]{1,0:T(8,128)(2,1)S(1)}, bf16[768,768]{1,0:T(8,128)(2,1)}, u32[]{:S(2)}) copy-start(bf16[768,768]{1,0:T(8,128)(2,1)} %all-gather.10.cloned.1.call-done) | copy-start | bytes 3538948
  472.8 62.2 %copy-start.3 = (bf16[768,768]{1,0:T(8,128)(2,1)S(1)}, bf16[768,768]{1,0:T(8,128)(2,1)}, u32[]{:S(2)}) copy-start(bf16[768,768]{1,0:T(8,128)(2,1)} %all-gather.12.cloned.1.call-done) | copy-start | bytes 3538948
  473.5 61.6 %copy-start.17 = (bf16[12,64,128]{2,1,0:T(8,128)(2,1)S(1)}, bf16[12,64,128]{2,1,0:T(8,128)(2,1)}, u32[]{:S(2)}) copy-start(bf16[12,64,128]{2,1,0:T(8,128)(2,1)} %copy-done.16) | copy-start | bytes 589828
  584.3 2.1 copy-start.22
  584.3 2.9 copy-start.21
  584.3 3.7 copy-start.20
  586.3 2.5 copy-start.7
  588.8 2.5 copy-start.6
  (5 other events, 6.4 us)
Sparse Core Ops, SparseCore 0:
  9.7 60.9 all-gather.9
  72.3 37.6 all-gather.11
  111.6 43.0 all-gather.7
  156.1 30.5 all-gather.13
  188.2 88.6 all-gather.15
  292.3 91.0 all-gather.17
  472.0 112.2 all-reduce.22
